TPU v7x, 512 devices: a whole 4x8x8 slice. The times are simulated.
512 devices in a mesh: wide: 64 (over y, x, z_hi), narrow: 8 (over z_lo, core).
Axes of the slice: x: 4, y: 8, z: 8 (z_hi: 2, z_lo: 4; z = z_hi * 4 + z_lo), core: 2. Of those that a mesh axis runs over, the one named last changes fastest.
Arguments:
- front: float32 [32768, 4096], P('wide', 'narrow'), as said below
- child_update: float32 [65536, 4096], P('wide', 'narrow'), may hold values from -0.8 to 0.8
- child_map: int32 [512], replicated, may hold values from -1 to 255, as said below
Outputs:
- factor: float32 [32768, 4096], P('wide', 'narrow')
Inputs may be any that keep to these rules, and one draw needn't show every extreme that they name: `child_map`: entry m names the global row block of the front into which child block m is added, or -1 for an empty block. With F = 4, blocks m from p * 2F to p * 2F + 2F - 1 lie on wide index p; those with p < 32 belong to the first child, the others to the second. The first F of them name blocks whose index mod 64 is p mod (32), the last F blocks whose index mod 64 is p mod (32) + 32; within each group of F the named blocks increase and the empty entries come last. Each child names 192 distinct blocks, and one front owner receives a full group from each child. `front`: entries lie within -0.8 and 0.8, except on the global diagonal of the first 512 global columns, where a value between 5 and 40 times the square root of 512 is added.
All inputs are finite; a program needn't handle non-finite values.
Results may differ from a plain program's by a relative error of at most 0.0001.
Values sent between devices are 32-bit elements; how exact they have to be, the bound alone decides.
A program may use at most 64 MiB of HBM per device.

v0:
```python
import jax
import jax.numpy as jnp
from jax import lax
from jax.sharding import Mesh
from jax.sharding import PartitionSpec as P

BS = 128
PW = 512
WIDE = ("wide_0", "wide_1", "wide_2")


HIGHEST_PRECISION = lax.Precision.HIGHEST


def from_partner(value, axis, distance):
    return lax.ppermute(value, axis, [(i, i ^ 1 << distance) for i in range(lax.axis_size(axis))])


def from_root(value, axis, root):
    return lax.dynamic_index_in_dim(lax.all_gather(value, axis), root, 0, keepdims=False)


def in_blocks(value, dim, size):
    before, after = (value.shape[:dim], value.shape[dim + 1 :])
    return jnp.moveaxis(value.reshape(*before, size, -1, *after), dim, 0)


def sent_and_summed(value, axis, dim):
    size = lax.axis_size(axis)
    pieces = lax.all_to_all(in_blocks(value, dim, size), axis, 0, 0, tiled=True)
    return jnp.sum(pieces, axis=0)


def padded_to(lines, size):
    spare = -lines.shape[0] % size
    if not spare:
        return lines
    return jnp.concatenate([lines, jnp.zeros((spare, *lines.shape[1:]), lines.dtype)])


def laid_out(pieces, dim):
    pieces = jnp.moveaxis(pieces, 0, dim)
    lengths = pieces.shape
    return pieces.reshape(*lengths[:dim], lengths[dim] * lengths[dim + 1], *lengths[dim + 2 :])


def copy_for_each(value, axis):
    size = lax.axis_size(axis)
    return lax.all_to_all(
        jnp.broadcast_to(value[None], (size, *value.shape)), axis, 0, 0, tiled=True
    )


def gathered_copies(value, axis, dim):
    return laid_out(copy_for_each(value, axis), dim)


def nested_sum(value, axes):
    lines = value.reshape(-1, value.shape[-1])
    own = sent_and_summed(padded_to(lines, lax.axis_size(axes)), axes, 0)
    whole = gathered_copies(own, axes, 0)
    return whole[: len(lines)].reshape(value.shape)


def spread(value, axes, root):
    value = jnp.where(lax.axis_index(axes) == root, value, jnp.zeros_like(value))
    for axis in axes:
        value = lax.psum(value, axis)
    return value


def right_solve(factor_diag, rows_in):
    return lax.linalg.triangular_solve(
        factor_diag, rows_in, left_side=False, lower=True, transpose_a=True
    )


def shards(front, child_update, child_map):
    wide_count = lax.axis_size(WIDE)
    narrow_count = lax.axis_size("narrow")
    wide_index = lax.axis_index(WIDE)
    narrow_index = lax.axis_index("narrow")
    half_count = wide_count // 2
    local_rows, local_cols = front.shape
    front_slots = local_rows // BS
    blocks_panel = PW // BS
    block_total = front_slots * wide_count
    child_side = wide_index // half_count
    row_local = jnp.arange(local_rows, dtype=jnp.int32)
    global_row = (row_local // BS * wide_count + wide_index) * BS + row_local % BS
    col_local = jnp.arange(local_cols, dtype=jnp.int32)
    global_col = (col_local // PW * narrow_count + narrow_index) * PW + col_local % PW
    child_names = lax.dynamic_slice_in_dim(child_map, child_side * block_total, block_total)
    named_cols = jnp.any(child_names[:, None] == (global_col // BS)[None, :], axis=0)
    groups = child_update.reshape(2, front_slots, BS, local_cols)
    groups = jnp.where(named_cols[None, None, None, :], groups, jnp.zeros_like(groups))
    kept_rows = lax.dynamic_index_in_dim(groups, child_side, 0, keepdims=False)
    leaving = lax.dynamic_index_in_dim(groups, 1 - child_side, 0, keepdims=False)
    arrived = from_partner(leaving, WIDE, half_count.bit_length() - 1)
    partner = (wide_index + half_count) % wide_count
    own_map = lax.dynamic_slice_in_dim(
        child_map, (wide_index * 2 + child_side) * front_slots, front_slots
    )
    got_map = lax.dynamic_slice_in_dim(
        child_map, (partner * 2 + child_side) * front_slots, front_slots
    )
    target = wide_index + wide_count * jnp.arange(front_slots, dtype=jnp.int32)
    own_select = (own_map[None, :] == target[:, None]).astype(jnp.float32)
    got_select = (got_map[None, :] == target[:, None]).astype(jnp.float32)
    own_part = jnp.dot(
        own_select,
        kept_rows.reshape(front_slots, BS * local_cols),
        precision=HIGHEST_PRECISION,
        preferred_element_type=jnp.float32,
    )
    got_part = jnp.dot(
        got_select,
        arrived.reshape(front_slots, BS * local_cols),
        precision=HIGHEST_PRECISION,
        preferred_element_type=jnp.float32,
    )
    matrix = front + (own_part + got_part).reshape(local_rows, local_cols)
    next_col = PW
    owner_col = 0 % narrow_count
    slot_col = 0 // narrow_count
    current = matrix
    panel_cols = from_root(current, "narrow", owner_col)
    shares = []
    for piece_index in range(blocks_panel):
        row_block = piece_index
        sender = row_block % wide_count
        row_slot = row_block // wide_count
        mine = panel_cols[row_slot * BS : (row_slot + 1) * BS]
        shares.append(jnp.where(wide_index == sender, mine, jnp.zeros_like(mine)))
    diag_block = nested_sum(jnp.concatenate(shares, 0), WIDE)
    symmetric = jnp.tril(diag_block) + jnp.tril(diag_block, -1).T
    factor_diag = jnp.tril(jnp.linalg.cholesky(symmetric))
    solved = right_solve(factor_diag, panel_cols)
    factor = jnp.where((global_row >= next_col)[:, None], solved, jnp.zeros_like(solved))
    for piece_index in range(blocks_panel):
        row_block = piece_index
        sender = row_block % wide_count
        row_slot = row_block // wide_count
        rows_here = factor_diag[piece_index * BS : (piece_index + 1) * BS]
        prior = factor[row_slot * BS : (row_slot + 1) * BS]
        factor = factor.at[row_slot * BS : (row_slot + 1) * BS].set(
            jnp.where(wide_index == sender, rows_here, prior)
        )
    written = jnp.where(narrow_index == owner_col, factor, current)
    matrix = matrix.at[:, slot_col * PW : (slot_col + 1) * PW].set(written)
    col_slot = 0
    column_block = narrow_index + narrow_count * col_slot
    pieces = []
    for piece_index in range(blocks_panel):
        row_block = column_block * blocks_panel + piece_index
        sender = row_block % wide_count
        row_slot = row_block // wide_count
        source = lax.dynamic_slice_in_dim(factor, row_slot * BS, BS)
        pieces.append(spread(source, WIDE, sender))
    panel_rows = [jnp.concatenate(pieces, 0)]
    col_slot = 0
    column_block = narrow_index + narrow_count * col_slot
    update = jnp.dot(
        factor,
        panel_rows[col_slot].T,
        precision=HIGHEST_PRECISION,
        preferred_element_type=jnp.float32,
    )
    segment = matrix
    renewed = jnp.where(column_block > 0, segment - update, segment)
    matrix = matrix.at[:, col_slot * PW : (col_slot + 1) * PW].set(renewed)
    on_or_below = global_row[:, None] >= global_col[None, :]
    return jnp.where(on_or_below, matrix, jnp.zeros_like(matrix))


def solution(mesh):
    torus = Mesh(
        mesh.devices.reshape(8, 4, 2, mesh.shape["narrow"]),
        ("wide_0", "wide_1", "wide_2", "narrow"),
    )
    placed = (P(WIDE, "narrow"), P(WIDE, "narrow"), P())
    return jax.shard_map(
        shards, mesh=torus, in_specs=placed, out_specs=P(WIDE, "narrow"), check_vma=False
    )
```

profile of v0, /device:TPU:1, one launch (start us, length us, event | category | flops | bytes accessed | tf_op | source)
XLA Modules:
  0.0 643.8 jit_solution(9065927038807821209)
XLA Ops:
  7.5 2.0 broadcast_select_fusion
  10.7 8.3 %collective-permute-start = (f32[4,128,512]{2,1,0:T(8,128)}, f32[4,128,512]{2,1,0:T(8,128)S(1)}, u32[]{:S(2)}, u32[]{:S(2)}) collective-permute-start(f32[4,128,512]{2,1,0:T(8,128)} %get-tuple-element.133), channel_id=1, source_target_pairs={{0,256},{8,264},{16,272},{24,280},{32,288},{40,296},{48,304},{56,3... | collective-permute-start | bytes 3145736 | tf_op jit(solution)/shard_map/ppermute | solution.py:16
  20.9 32.3 %collective-permute-done = f32[4,128,512]{2,1,0:T(8,128)S(1)} collective-permute-done((f32[4,128,512]{2,1,0:T(8,128)}, f32[4,128,512]{2,1,0:T(8,128)S(1)}, u32[]{:S(2)}, u32[]{:S(2)}) %collective-permute-start) | collective-permute-done | bytes 1048608 | tf_op jit(solution)/shard_map/ppermute | solution.py:16
  55.9 2.4 add.301
  58.4 111.1 %all-gather.3.cloned.1.call-done = f32[4096,512]{1,0:T(8,128)} async-done(((f32[512,512]{1,0:T(8,128)}), f32[4096,512]{1,0:T(8,128)}) %all-gather.3.cloned.1.call-update) | async-done | bytes 8388624 | tf_op jit(solution)/shard_map/all_gather | solution.py:20
  170.6 45.7 %all_to_all.10 = f32[64,8,512]{2,1,0:T(8,128)S(1)} all-to-all(f32[64,8,512]{2,1,0:T(8,128)S(1)} %maximum_bitcast_fusion), channel_id=1, replica_groups=mesh['wide_0'=8,'wide_1'=4,'wide_2'=2,'narrow'=8] {'wide_0','wide_1','wi..., dimensions={0} | all-to-all | bytes 2097152 | tf_op jit(solution)/shard_map/all_to_all | solution.py:30
  217.6 7.8 %all-to-all-start.1 = ((f32[64,8,512]{2,1,0:T(8,128)}), f32[64,8,512]{2,1,0:T(8,128)S(1)}, u32[]{:S(2)}, u32[]{:S(2)}) async-start(f32[64,8,512]{2,1,0:T(8,128)} %broadcast_in_dim.32), calls=%async_computation.1 | async-start | bytes 2097152 | tf_op jit(solution)/shard_map/all_to_all | solution.py:49
  226.0 29.4 %all-to-all-done.1 = f32[64,8,512]{2,1,0:T(8,128)S(1)} async-done(((f32[64,8,512]{2,1,0:T(8,128)}), f32[64,8,512]{2,1,0:T(8,128)S(1)}, u32[]{:S(2)}, u32[]{:S(2)}) %all-to-all-start.1) | async-done | bytes 1048608 | tf_op jit(solution)/shard_map/all_to_all | solution.py:49
  256.6 11.7 %cholesky.103 = f32[128,128]{1,0:T(8,128)S(1)} custom-call(f32[128,128]{1,0:T(8,128)S(1)} %cholesky.263), custom_call_target="Cholesky" | custom-call | tf_op jit(solution)/shard_map/jit(cholesky)/cholesky | solution.py:137
  268.5 9.8 %custom-call.30 = f32[1,128,128]{1,2,0:T(8,128)S(1)} custom-call(f32[1,128,128]{2,1,0:T(8,128)S(1)} %get-tuple-element.148), custom_call_target="InvertDiagBlocksLowerTriangular" | custom-call | tf_op jit(solution)/shard_map/jit(cholesky)/cholesky | solution.py:137
  279.0 11.7 %cholesky.215 = f32[128,128]{1,0:T(8,128)S(1)} custom-call(f32[128,128]{1,0:T(8,128)S(1)} %cholesky.267), custom_call_target="Cholesky" | custom-call | tf_op jit(solution)/shard_map/jit(cholesky)/cholesky | solution.py:137
  292.0 10.0 %custom-call.31 = f32[1,128,128]{1,2,0:T(8,128)S(1)} custom-call(f32[1,128,128]{2,1,0:T(8,128)S(1)} %get-tuple-element.145), custom_call_target="InvertDiagBlocksLowerTriangular" | custom-call | tf_op jit(solution)/shard_map/jit(cholesky)/cholesky | solution.py:137
  302.7 11.7 %cholesky.236 = f32[128,128]{1,0:T(8,128)S(1)} custom-call(f32[128,128]{1,0:T(8,128)S(1)} %cholesky.272), custom_call_target="Cholesky" | custom-call | tf_op jit(solution)/shard_map/jit(cholesky)/cholesky | solution.py:137
  315.0 9.8 %custom-call.32 = f32[1,128,128]{1,2,0:T(8,128)S(1)} custom-call(f32[1,128,128]{2,1,0:T(8,128)S(1)} %get-tuple-element.142), custom_call_target="InvertDiagBlocksLowerTriangular" | custom-call | tf_op jit(solution)/shard_map/jit(cholesky)/cholesky | solution.py:137
  325.4 11.9 %cholesky.253 = f32[128,128]{1,0:T(8,128)S(1)} custom-call(f32[128,128]{1,0:T(8,128)S(1)} %convolution_subtract_fusion.5), custom_call_target="Cholesky" | custom-call | tf_op jit(solution)/shard_map/jit(cholesky)/cholesky | solution.py:137
  340.8 10.0 %while.9 = (s32[]{:T(128)}, f32[512,512]{1,0:T(8,128)S(1)}, s32[4,2]{0,1:T(2,128)S(1)}, f32[4,128,128]{2,1,0:T(8,128)}, s32[]{:T(128)}) while((s32[]{:T(128)}, f32[512,512]{1,0:T(8,128)S(1)}, s32[4,2]{0,1:T(2,128)S(1)}, f32[4,128,128]{2,1,0:T(8,128)}, s32[]{:T(128)}) %tuple.69), condition=%wide.while_cond.6, body=%wide.while_body.6.sunk | while | flops 2 | bytes 132705 | solution.py:73
  343.9 1.9 bitcast_dynamic-update-slice_fusion.2
  351.9 40.1 %custom-call.33 = f32[4,128,128]{1,2,0:T(8,128)S(1)} custom-call(f32[4,128,128]{2,1,0:T(8,128)} %get-tuple-element.100), custom_call_target="InvertDiagBlocksLowerTriangular" | custom-call | tf_op jit(solution)/shard_map/triangular_solve | solution.py:73
  397.4 2.0 convolution_subtract_fusion
  401.5 2.5 convolution_subtract_fusion.2
  407.8 73.7 %all-reduce.8.cloned.1.call-done = (f32[128,512]{1,0:T(8,128)}, f32[128,512]{1,0:T(8,128)}, f32[128,512]{1,0:T(8,128)}, f32[128,512]{1,0:T(8,128)}) async-done(((f32[128,512]{1,0:T(8,128)}, f32[128,512]{1,0:T(8,128)}, f32[128,512]{1,0:T(8,128)}, f32[128,512]{1,0:T(8,128)}), (f32[128,512]{1,0:T(8,128)}, f32[128,512]{1,0:T(8,128)}, f32[128,512]{1,0:T(8,128)}, ...) | async-done | bytes 1048592 | tf_op jit(solution)/shard_map/psum | solution.py:68
  481.6 60.5 %all-reduce.10.cloned.1.call-done = (f32[128,512]{1,0:T(8,128)}, f32[128,512]{1,0:T(8,128)}, f32[128,512]{1,0:T(8,128)}, f32[128,512]{1,0:T(8,128)}) async-done(((f32[128,512]{1,0:T(8,128)}, f32[128,512]{1,0:T(8,128)}, f32[128,512]{1,0:T(8,128)}, f32[128,512]{1,0:T(8,128)}), (f32[128,512]{1,0:T(8,128)}, f32[128,512]{1,0:T(8,128)}, f32[128,512]{1,0:T(8,128)}, ...) | async-done | bytes 1048592 | tf_op jit(solution)/shard_map/psum | solution.py:68
  542.1 90.9 %all-reduce.12.cloned.1.call-done = (f32[128,512]{1,0:T(8,128)}, f32[128,512]{1,0:T(8,128)}, f32[128,512]{1,0:T(8,128)}, f32[128,512]{1,0:T(8,128)}) async-done(((f32[128,512]{1,0:T(8,128)}, f32[128,512]{1,0:T(8,128)}, f32[128,512]{1,0:T(8,128)}, f32[128,512]{1,0:T(8,128)}), (f32[128,512]{1,0:T(8,128)}, f32[128,512]{1,0:T(8,128)}, f32[128,512]{1,0:T(8,128)}, ...) | async-done | bytes 1048592 | tf_op jit(solution)/shard_map/psum | solution.py:68
  632.9 4.1 fusion
  (85 shorter events, 36.3 us)
Async XLA Ops:
  6.5 13.2 %copy-start.3 = (s32[512]{0:T(512)S(1)}, s32[512]{0:T(512)}, u32[]{:S(2)}) copy-start(s32[512]{0:T(512)} %param.21) | copy-start | bytes 6148
  6.5 162.9 %all-gather.3.cloned.1.call-start = ((), (), s32[]{:S(2)}) async-start(), calls=%async_computation.2 | async-start | bytes 9437184 | tf_op jit(solution)/shard_map/all_gather | solution.py:20
  10.7 42.5 %collective-permute-start = (f32[4,128,512]{2,1,0:T(8,128)}, f32[4,128,512]{2,1,0:T(8,128)S(1)}, u32[]{:S(2)}, u32[]{:S(2)}) collective-permute-start(f32[4,128,512]{2,1,0:T(8,128)} %get-tuple-element.133), channel_id=1, source_target_pairs={{0,256},{8,264},{16,272},{24,280},{32,288},{40,296},{48,304},{56,3... | collective-permute-start | bytes 3145736 | tf_op jit(solution)/shard_map/ppermute | solution.py:16
  217.6 37.8 %all-to-all-start.1 = ((f32[64,8,512]{2,1,0:T(8,128)}), f32[64,8,512]{2,1,0:T(8,128)S(1)}, u32[]{:S(2)}, u32[]{:S(2)}) async-start(f32[64,8,512]{2,1,0:T(8,128)} %broadcast_in_dim.32), calls=%async_computation.1 | async-start | bytes 2097152 | tf_op jit(solution)/shard_map/all_to_all | solution.py:49
  225.4 256.1 %all-reduce.8.cloned.1.call-start = ((), (), s32[]{:S(2)}) async-start(), calls=%async_computation.3 | async-start | bytes 2097152 | tf_op jit(solution)/shard_map/psum | solution.py:68
  350.8 1.0 copy-start.1
  392.0 1.6 copy-start.2
  395.2 237.7 %copy-start = (f32[512,512]{1,0:T(8,128)S(1)}, f32[512,512]{1,0:T(8,128)}, u32[]{:S(2)}) copy-start(f32[512,512]{1,0:T(8,128)} %add.301) | copy-start | bytes 3145732
  407.8 134.3 %all-reduce.10.cloned.1.call-start = ((), (), s32[]{:S(2)}) async-start(), calls=%async_computation.4 | async-start | bytes 2097152 | tf_op jit(solution)/shard_map/psum | solution.py:68
  481.5 151.4 %all-reduce.12.cloned.1.call-start = ((), (), s32[]{:S(2)}) async-start(), calls=%async_computation.5 | async-start | bytes 2097152 | tf_op jit(solution)/shard_map/psum | solution.py:68
Sparse Core Ops, SparseCore 0:
  58.5 110.9 all-gather.2
  407.9 73.5 all-reduce.7
  484.0 57.9 all-reduce.9
  545.3 87.6 all-reduce.11
where the time goes:
time: 651 us; the launch traced here: 644 us
  waiting for transfers between devices  398 us (61%)
  other arithmetic  129 us (20%)
  blocking collectives  45.7 us (7%)
  matrix products  19.7 us (3%)
  local copies, waits for them, and re-layouts  19 us (3%)
  starting transfers between devices  16.7 us (3%)
  between operations  16.3 us (3%)
    psum x3, waiting for transfers between devices, spread(): value = lax.psum(value, axis)  225 us
    all_gather x1, waiting for transfers between devices, from_root(): lax.all_gather(value, axis)  111 us
    another operation x15, other arithmetic, shards(): factor_diag = jnp.tril(jnp.linalg.cholesky(symmetric))  79.4 us
    all_to_all x1, blocking collectives, sent_and_summed(): pieces = lax.all_to_all(in_blocks(value, dim, size), axis, 0, 0, tiled=True)  45.7 us
    another operation x3, other arithmetic, right_solve(): lax.linalg.triangular_solve(factor_diag, rows_in, left_side=False, lower=...  40.4 us
    ppermute x1, waiting for transfers between devices, from_partner(): lax.ppermute(value, axis, [(i, i ^ 1 << distance) for i in range(lax.axis...  32.3 us
    all_to_all x1, waiting for transfers between devices, copy_for_each(): lax.all_to_all(jnp.broadcast_to(value[None], (size, *value.shape)), axis,...  29.4 us
  transfers between devices with their start and end apart: 6, of which 6 were waited for; matrix products, arithmetic and copies ran while one was open for 0% of the time, Pallas kernels for 0%

commit v1 on v0

v1 whole, which is shorter than its diff:
```python
import functools

import jax
import jax.numpy as jnp
from jax import lax
from jax.experimental import pallas as pl
from jax.experimental.pallas import tpu as pltpu
from jax.sharding import Mesh
from jax.sharding import PartitionSpec as P

BS = 128
PW = 512
WIDE = ("wide_0", "wide_1", "wide_2")
AXES = ("wide_0", "wide_1", "wide_2", "narrow")
MESH_ID = pl.DeviceIdType.MESH

HIGHEST_PRECISION = lax.Precision.HIGHEST


def from_partner(value, axis, distance):
    return lax.ppermute(value, axis, [(i, i ^ 1 << distance) for i in range(lax.axis_size(axis))])


def positions():
    return tuple(lax.axis_index(a) for a in AXES)


NARROW_CHUNKS = 4


def narrow_bcast_kernel(src_ref, out_ref, send_sem, recv_sem):
    y, x, h, q = positions()
    n = lax.axis_size("narrow")
    rows = out_ref.shape[0] // NARROW_CHUNKS
    even = q % 2 == 0
    has_parent = q > 0
    parent = jnp.where(even, q - 2, q - 1)
    kids = [(even, q + 1), (jnp.logical_and(even, q + 2 < n), q + 2)]

    barrier = pltpu.get_barrier_semaphore()

    @pl.when(has_parent)
    def _():
        pl.semaphore_signal(barrier, 1, device_id=(y, x, h, parent), device_id_type=MESH_ID)

    for cond, kid in kids:
        @pl.when(cond)
        def _():
            pl.semaphore_signal(barrier, 1, device_id=(y, x, h, kid), device_id_type=MESH_ID)

    peers = has_parent.astype(jnp.int32)
    for cond, kid in kids:
        peers = peers + cond.astype(jnp.int32)
    pl.semaphore_wait(barrier, peers)

    @pl.when(q == 0)
    def _():
        out_ref[...] = src_ref[...]

    def copy(src, c, k, kid):
        part = pl.ds(c * rows, rows)
        return pltpu.make_async_remote_copy(
            src_ref=src.at[part],
            dst_ref=out_ref.at[part],
            send_sem=send_sem.at[c, k],
            recv_sem=recv_sem.at[c],
            device_id=(y, x, h, kid),
            device_id_type=MESH_ID,
        )

    for c in range(NARROW_CHUNKS):
        @pl.when(has_parent)
        def _():
            copy(out_ref, c, 0, q).wait_recv()

        for k, (cond, kid) in enumerate(kids):
            @pl.when(jnp.logical_and(cond, q == 0))
            def _():
                copy(src_ref, c, k, kid).start()

            @pl.when(jnp.logical_and(cond, q != 0))
            def _():
                copy(out_ref, c, k, kid).start()

    for c in range(NARROW_CHUNKS):
        for k, (cond, kid) in enumerate(kids):
            @pl.when(cond)
            def _():
                copy(out_ref, c, k, kid).wait_send()


def narrow_bcast(panel):
    return pl.pallas_call(
        narrow_bcast_kernel,
        out_shape=jax.ShapeDtypeStruct(panel.shape, panel.dtype),
        in_specs=[pl.BlockSpec(memory_space=pltpu.VMEM)],
        out_specs=pl.BlockSpec(memory_space=pltpu.VMEM),
        scratch_shapes=[
            pltpu.SemaphoreType.DMA((NARROW_CHUNKS, 2)),
            pltpu.SemaphoreType.DMA((NARROW_CHUNKS,)),
        ],
        compiler_params=pltpu.CompilerParams(collective_id=0, has_side_effects=True),
    )(panel)


WIDE_CHUNKS = 4
N_BLOCKS = 8
N_SLOTS = 6


def wide_tree(y, x, h, root, ny, nx):
    y0 = root // (2 * nx)
    x0 = (root // 2) % nx
    h0 = root % 2
    dy = (y - y0 + ny) % ny
    dx = (x - x0 + nx) % nx
    dh = (h - h0 + 2) % 2
    half = ny // 2
    at_y0 = dy == 0
    at_x0 = jnp.logical_and(at_y0, dx == 0)
    is_root = jnp.logical_and(at_x0, dh == 0)
    up = jnp.logical_and(dy >= 1, dy <= half)
    py = jnp.where(up, (y + ny - 1) % ny, (y + 1) % ny)
    px = jnp.where(dx == 2, (x + nx - 1) % nx, x0)
    parent_y = jnp.where(at_y0, y, py)
    parent_x = jnp.where(jnp.logical_and(at_y0, dx != 0), px, x)
    parent_h = jnp.where(at_x0, h0, h)
    parent = (parent_y, parent_x, parent_h)
    kids = [
        (is_root, (y, x, 1 - h)),
        (at_x0, (y, (x + 1) % nx, h)),
        (at_x0, (y, (x + nx - 1) % nx, h)),
        (jnp.logical_and(at_y0, dx == 1), (y, (x + 1) % nx, h)),
        (dy < half, ((y + 1) % ny, x, h)),
        (jnp.logical_or(at_y0, dy > half + 1), ((y + ny - 1) % ny, x, h)),
    ]
    return is_root, parent, kids


def wide_bcast_kernel(src_ref, out_ref, send_sem, recv_sem):
    y, x, h, q = positions()
    ny = lax.axis_size("wide_0")
    nx = lax.axis_size("wide_1")
    rows = src_ref.shape[0] // WIDE_CHUNKS
    me = (y * nx + x) * 2 + h
    trees = []
    for j in range(N_BLOCKS):
        if j < N_BLOCKS // 2:
            root = j
            active = q >= 0
        else:
            root = 4 * q + (j - N_BLOCKS // 2)
            active = q > 0
        is_root, parent, kids = wide_tree(y, x, h, root, ny, nx)
        trees.append((active, is_root, parent, kids))

    barrier = pltpu.get_barrier_semaphore()
    for active, is_root, parent, kids in trees:
        @pl.when(jnp.logical_and(active, jnp.logical_not(is_root)))
        def _():
            pl.semaphore_signal(barrier, 1, device_id=(*parent, q), device_id_type=MESH_ID)

        for cond, kid in kids:
            @pl.when(jnp.logical_and(active, cond))
            def _():
                pl.semaphore_signal(barrier, 1, device_id=(*kid, q), device_id_type=MESH_ID)

    peers = jnp.int32(0)
    for active, is_root, parent, kids in trees:
        peers = peers + jnp.logical_and(active, jnp.logical_not(is_root)).astype(jnp.int32)
        for cond, kid in kids:
            peers = peers + jnp.logical_and(active, cond).astype(jnp.int32)
    pl.semaphore_wait(barrier, peers)

    for j, (active, is_root, parent, kids) in enumerate(trees):
        @pl.when(jnp.logical_and(active, is_root))
        def _():
            out_ref[j] = src_ref[...]

    def copy(src, j, c, k, kid):
        part = pl.ds(c * rows, rows)
        return pltpu.make_async_remote_copy(
            src_ref=src.at[part],
            dst_ref=out_ref.at[j, part],
            send_sem=send_sem.at[j, c, k],
            recv_sem=recv_sem.at[j, c],
            device_id=(*kid, q),
            device_id_type=MESH_ID,
        )

    for c in range(WIDE_CHUNKS):
        for j, (active, is_root, parent, kids) in enumerate(trees):
            @pl.when(jnp.logical_and(active, jnp.logical_not(is_root)))
            def _():
                copy(out_ref.at[j], j, c, 0, (y, x, h)).wait_recv()

            for k, (cond, kid) in enumerate(kids):
                go = jnp.logical_and(active, cond)

                @pl.when(jnp.logical_and(go, is_root))
                def _():
                    copy(src_ref, j, c, k, kid).start()

                @pl.when(jnp.logical_and(go, jnp.logical_not(is_root)))
                def _():
                    copy(out_ref.at[j], j, c, k, kid).start()

    for c in range(WIDE_CHUNKS):
        for j, (active, is_root, parent, kids) in enumerate(trees):
            for k, (cond, kid) in enumerate(kids):
                @pl.when(jnp.logical_and(active, cond))
                def _():
                    copy(out_ref.at[j], j, c, k, kid).wait_send()


def wide_bcast(block):
    return pl.pallas_call(
        wide_bcast_kernel,
        out_shape=jax.ShapeDtypeStruct((N_BLOCKS, *block.shape), block.dtype),
        in_specs=[pl.BlockSpec(memory_space=pltpu.VMEM)],
        out_specs=pl.BlockSpec(memory_space=pltpu.VMEM),
        scratch_shapes=[
            pltpu.SemaphoreType.DMA((N_BLOCKS, WIDE_CHUNKS, N_SLOTS)),
            pltpu.SemaphoreType.DMA((N_BLOCKS, WIDE_CHUNKS)),
        ],
        compiler_params=pltpu.CompilerParams(collective_id=1, has_side_effects=True),
    )(block)


def mm_t(a, b):
    return lax.dot_general(
        a, b, (((1,), (1,)), ((), ())),
        precision=HIGHEST_PRECISION, preferred_element_type=jnp.float32,
    )


def shards(front, child_update, child_map):
    wide_count = lax.axis_size(WIDE)
    narrow_count = lax.axis_size("narrow")
    wide_index = lax.axis_index(WIDE)
    narrow_index = lax.axis_index("narrow")
    half_count = wide_count // 2
    local_rows, local_cols = front.shape
    front_slots = local_rows // BS
    block_total = front_slots * wide_count
    child_side = wide_index // half_count
    row_local = jnp.arange(local_rows, dtype=jnp.int32)
    global_row = (row_local // BS * wide_count + wide_index) * BS + row_local % BS
    col_local = jnp.arange(local_cols, dtype=jnp.int32)
    global_col = (col_local // PW * narrow_count + narrow_index) * PW + col_local % PW
    child_names = lax.dynamic_slice_in_dim(child_map, child_side * block_total, block_total)
    named_cols = jnp.any(child_names[:, None] == (global_col // BS)[None, :], axis=0)
    groups = child_update.reshape(2, front_slots, BS, local_cols)
    groups = jnp.where(named_cols[None, None, None, :], groups, jnp.zeros_like(groups))
    kept_rows = lax.dynamic_index_in_dim(groups, child_side, 0, keepdims=False)
    leaving = lax.dynamic_index_in_dim(groups, 1 - child_side, 0, keepdims=False)
    arrived = from_partner(leaving, WIDE, half_count.bit_length() - 1)
    partner = (wide_index + half_count) % wide_count
    own_map = lax.dynamic_slice_in_dim(
        child_map, (wide_index * 2 + child_side) * front_slots, front_slots
    )
    got_map = lax.dynamic_slice_in_dim(
        child_map, (partner * 2 + child_side) * front_slots, front_slots
    )
    target = wide_index + wide_count * jnp.arange(front_slots, dtype=jnp.int32)
    own_select = (own_map[None, :] == target[:, None]).astype(jnp.float32)
    got_select = (got_map[None, :] == target[:, None]).astype(jnp.float32)
    own_part = jnp.dot(
        own_select,
        kept_rows.reshape(front_slots, BS * local_cols),
        precision=HIGHEST_PRECISION,
        preferred_element_type=jnp.float32,
    )
    got_part = jnp.dot(
        got_select,
        arrived.reshape(front_slots, BS * local_cols),
        precision=HIGHEST_PRECISION,
        preferred_element_type=jnp.float32,
    )
    matrix = front + (own_part + got_part).reshape(local_rows, local_cols)

    panel = narrow_bcast(matrix)
    blocks = wide_bcast(panel[:BS])
    diag_block = blocks[: N_BLOCKS // 2].reshape(PW, PW)
    col_rows = blocks[N_BLOCKS // 2 :].reshape(PW, PW)

    symmetric = jnp.tril(diag_block) + jnp.tril(diag_block, -1).T
    factor_diag = jnp.tril(jnp.linalg.cholesky(symmetric))
    inverse = lax.linalg.triangular_solve(
        factor_diag, jnp.eye(PW, dtype=jnp.float32), left_side=True, lower=True
    )
    own_factor = mm_t(panel, inverse)
    diag_rows = lax.dynamic_slice_in_dim(factor_diag, jnp.minimum(wide_index, 3) * BS, BS)
    top = jnp.where(wide_index * BS < PW, diag_rows, own_factor[:BS])
    own_factor = jnp.concatenate([top, own_factor[BS:]], 0)
    col_factor = mm_t(col_rows, inverse)
    update = mm_t(own_factor, col_factor)
    renewed = jnp.where(narrow_index == 0, own_factor, matrix - update)
    on_or_below = global_row[:, None] >= global_col[None, :]
    return jnp.where(on_or_below, renewed, jnp.zeros_like(renewed))


def solution(mesh):
    torus = Mesh(
        mesh.devices.reshape(8, 4, 2, mesh.shape["narrow"]),
        AXES,
    )
    placed = (P(WIDE, "narrow"), P(WIDE, "narrow"), P())
    return jax.shard_map(
        shards, mesh=torus, in_specs=placed, out_specs=P(WIDE, "narrow"), check_vma=False
    )
```

time: 651 us -> 577 us (0.89)
  the two profiles are of different devices: /device:TPU:1 before, /device:TPU:254 now
where the time goes in v1:
time: 577 us; the launch traced here: 571 us
  Pallas kernels  344 us (60%)
  other arithmetic  129 us (22%)
  waiting for transfers between devices  44 us (8%)
  local copies, waits for them, and re-layouts  24.6 us (4%)
  matrix products  21.8 us (4%)
    pallas_call x1, Pallas kernels, wide_bcast(): pl.pallas_call(wide_bcast_kernel, out_shape=jax.ShapeDtypeStruct((N_BLOCK...  317 us
    another operation x15, other arithmetic, shards(): factor_diag = jnp.tril(jnp.linalg.cholesky(symmetric))  79.4 us
    ppermute x1, waiting for transfers between devices, from_partner(): lax.ppermute(value, axis, [(i, i ^ 1 << distance) for i in range(lax.axis...  44 us
    another operation x3, other arithmetic, shards(): lax.linalg.triangular_solve(factor_diag, jnp.eye(PW, dtype=jnp.float32),...  41.7 us
    pallas_call x1, Pallas kernels, narrow_bcast(): pl.pallas_call(narrow_bcast_kernel, out_shape=jax.ShapeDtypeStruct(panel....  27 us
    another operation x12, local copies, waits for them, and re-layouts  14.1 us
  transfers between devices with their start and end apart: 1, of which 1 were waited for; matrix products, arithmetic and copies ran while one was open for 1% of the time, Pallas kernels for 0%

profile of v1, /device:TPU:254, one launch (start us, length us, event | category | flops | bytes accessed | tf_op | source)
XLA Modules:
  0.0 570.8 jit_solution(778149779935996312)
XLA Ops:
  0.9 2.0 broadcast_select_fusion
  4.2 4.8 collective-permute-start
  12.2 44.0 %collective-permute-done = f32[4,128,512]{2,1,0:T(8,128)S(1)} collective-permute-done((f32[4,128,512]{2,1,0:T(8,128)}, f32[4,128,512]{2,1,0:T(8,128)S(1)}, u32[]{:S(2)}, u32[]{:S(2)}) %collective-permute-start) | collective-permute-done | bytes 1048608 | tf_op jit(solution)/shard_map/ppermute | solution.py:21
  60.1 27.0 %shard_map.37 = f32[512,512]{1,0:T(8,128)} custom-call(f32[512,512]{1,0:T(8,128)} %add.207.src_ref), custom_call_target="tpu_custom_call" | custom-call | tf_op jit(solution)/shard_map/pallas_call | solution.py:93
  87.1 1.7 slice.118.src_ref
  88.8 316.7 %shard_map.38 = f32[8,128,512]{2,1,0:T(8,128)} custom-call(f32[128,512]{1,0:T(8,128)} %slice.118.src_ref), custom_call_target="tpu_custom_call" | custom-call | tf_op jit(solution)/shard_map/pallas_call | solution.py:217
  405.5 1.8 fusion.69
  411.8 11.7 %cholesky.103 = f32[128,128]{1,0:T(8,128)S(1)} custom-call(f32[128,128]{1,0:T(8,128)S(1)} %cholesky.263), custom_call_target="Cholesky" | custom-call | tf_op jit(solution)/shard_map/jit(cholesky)/cholesky | solution.py:288
  423.7 9.8 %custom-call.30 = f32[1,128,128]{1,2,0:T(8,128)S(1)} custom-call(f32[1,128,128]{2,1,0:T(8,128)S(1)} %get-tuple-element.38), custom_call_target="InvertDiagBlocksLowerTriangular" | custom-call | tf_op jit(solution)/shard_map/jit(cholesky)/cholesky | solution.py:288
  436.0 11.9 %cholesky.215 = f32[128,128]{1,0:T(8,128)S(1)} custom-call(f32[128,128]{1,0:T(8,128)S(1)} %cholesky.267), custom_call_target="Cholesky" | custom-call | tf_op jit(solution)/shard_map/jit(cholesky)/cholesky | solution.py:288
  447.9 9.8 %custom-call.31 = f32[1,128,128]{1,2,0:T(8,128)S(1)} custom-call(f32[1,128,128]{2,1,0:T(8,128)S(1)} %get-tuple-element.35), custom_call_target="InvertDiagBlocksLowerTriangular" | custom-call | tf_op jit(solution)/shard_map/jit(cholesky)/cholesky | solution.py:288
  459.3 11.7 %cholesky.236 = f32[128,128]{1,0:T(8,128)S(1)} custom-call(f32[128,128]{1,0:T(8,128)S(1)} %cholesky.272), custom_call_target="Cholesky" | custom-call | tf_op jit(solution)/shard_map/jit(cholesky)/cholesky | solution.py:288
  471.0 9.8 %custom-call.32 = f32[1,128,128]{1,2,0:T(8,128)S(1)} custom-call(f32[1,128,128]{2,1,0:T(8,128)S(1)} %get-tuple-element.32), custom_call_target="InvertDiagBlocksLowerTriangular" | custom-call | tf_op jit(solution)/shard_map/jit(cholesky)/cholesky | solution.py:288
  482.3 11.9 %cholesky.253 = f32[128,128]{1,0:T(8,128)S(1)} custom-call(f32[128,128]{1,0:T(8,128)S(1)} %convolution_subtract_fusion.6), custom_call_target="Cholesky" | custom-call | tf_op jit(solution)/shard_map/jit(cholesky)/cholesky | solution.py:288
  499.4 1.6 fusion.6
  501.1 14.2 %while.1 = (s32[]{:T(128)}, f32[512,512]{1,0:T(8,128)}, s32[4,2]{0,1:T(2,128)S(1)}, f32[4,128,128]{2,1,0:T(8,128)}, s32[]{:T(128)}) while((s32[]{:T(128)}, f32[512,512]{1,0:T(8,128)}, s32[4,2]{0,1:T(2,128)S(1)}, f32[4,128,128]{2,1,0:T(8,128)}, s32[]{:T(128)}) %tuple.32), condition=%wide.while_cond, body=%wide.while_body.sunk | while | flops 2 | bytes 132205 | solution.py:289
  501.7 2.9 bitcast_dynamic-update-slice_fusion.2
  505.3 2.9 bitcast_dynamic-update-slice_fusion.2
  508.8 2.9 bitcast_dynamic-update-slice_fusion.2
  512.4 2.8 bitcast_dynamic-update-slice_fusion.2
  515.2 40.1 %custom-call.33 = f32[4,128,128]{1,2,0:T(8,128)S(1)} custom-call(f32[4,128,128]{2,1,0:T(8,128)} %get-tuple-element.12), custom_call_target="InvertDiagBlocksLowerTriangular" | custom-call | tf_op jit(solution)/shard_map/triangular_solve | solution.py:289
  562.8 1.9 fusion.13
  564.7 1.9 fusion.12
  567.6 2.9 fusion.1
  (72 shorter events, 33.0 us)
Async XLA Ops:
  4.1 5.6 copy-start.6
  4.2 52.0 %collective-permute-start = (f32[4,128,512]{2,1,0:T(8,128)}, f32[4,128,512]{2,1,0:T(8,128)S(1)}, u32[]{:S(2)}, u32[]{:S(2)}) collective-permute-start(f32[4,128,512]{2,1,0:T(8,128)} %get-tuple-element.27), channel_id=1, source_target_pairs={{0,256},{8,264},{16,272},{24,280},{32,288},{40,296},{48,304},{56,3... | collective-permute-start | bytes 3145736 | tf_op jit(solution)/shard_map/ppermute | solution.py:21
  56.9 2.0 copy-start.4
  410.8 1.0 copy-start.3
  499.4 56.3 %copy-start.2 = (f32[512,512]{1,0:T(8,128)S(1)}, f32[512,512]{1,0:T(8,128)}, u32[]{:S(2)}) copy-start(f32[512,512]{1,0:T(8,128)} %fusion.17) | copy-start | bytes 3145732
  555.3 1.6 copy-start.5
  556.9 5.9 %copy-start.1 = (f32[512,512]{1,0:T(8,128)S(1)}, f32[512,512]{1,0:T(8,128)}, u32[]{:S(2)}) copy-start(f32[512,512]{1,0:T(8,128)} %shard_map.37) | copy-start | bytes 3145732
  564.7 3.0 copy-start

commit v2 on v1

--- a/solution.py
+++ b/solution.py
@@ -103,9 +103,9 @@
     )(panel)
 
 
-WIDE_CHUNKS = 4
 N_BLOCKS = 8
 N_SLOTS = 6
+MAX_DEPTH = 8
 
 
 def wide_tree(y, x, h, root, ny, nx):
@@ -134,15 +134,16 @@
         (dy < half, ((y + 1) % ny, x, h)),
         (jnp.logical_or(at_y0, dy > half + 1), ((y + ny - 1) % ny, x, h)),
     ]
-    return is_root, parent, kids
+    x_depth = jnp.where(dx == 0, 0, jnp.where(dx == 2, 2, 1))
+    y_depth = jnp.where(dy <= half, dy, ny - dy)
+    depth = dh + x_depth + y_depth
+    return is_root, parent, kids, depth
 
 
 def wide_bcast_kernel(src_ref, out_ref, send_sem, recv_sem):
     y, x, h, q = positions()
     ny = lax.axis_size("wide_0")
     nx = lax.axis_size("wide_1")
-    rows = src_ref.shape[0] // WIDE_CHUNKS
-    me = (y * nx + x) * 2 + h
     trees = []
     for j in range(N_BLOCKS):
         if j < N_BLOCKS // 2:
@@ -151,11 +152,11 @@
         else:
             root = 4 * q + (j - N_BLOCKS // 2)
             active = q > 0
-        is_root, parent, kids = wide_tree(y, x, h, root, ny, nx)
-        trees.append((active, is_root, parent, kids))
+        is_root, parent, kids, depth = wide_tree(y, x, h, root, ny, nx)
+        trees.append((active, is_root, parent, kids, depth))
 
     barrier = pltpu.get_barrier_semaphore()
-    for active, is_root, parent, kids in trees:
+    for active, is_root, parent, kids, depth in trees:
         @pl.when(jnp.logical_and(active, jnp.logical_not(is_root)))
         def _():
             pl.semaphore_signal(barrier, 1, device_id=(*parent, q), device_id_type=MESH_ID)
@@ -166,51 +167,52 @@
                 pl.semaphore_signal(barrier, 1, device_id=(*kid, q), device_id_type=MESH_ID)
 
     peers = jnp.int32(0)
-    for active, is_root, parent, kids in trees:
+    for active, is_root, parent, kids, depth in trees:
         peers = peers + jnp.logical_and(active, jnp.logical_not(is_root)).astype(jnp.int32)
         for cond, kid in kids:
             peers = peers + jnp.logical_and(active, cond).astype(jnp.int32)
     pl.semaphore_wait(barrier, peers)
 
-    for j, (active, is_root, parent, kids) in enumerate(trees):
-        @pl.when(jnp.logical_and(active, is_root))
-        def _():
-            out_ref[j] = src_ref[...]
-
-    def copy(src, j, c, k, kid):
-        part = pl.ds(c * rows, rows)
+    def copy(src, j, k, kid):
         return pltpu.make_async_remote_copy(
-            src_ref=src.at[part],
-            dst_ref=out_ref.at[j, part],
-            send_sem=send_sem.at[j, c, k],
-            recv_sem=recv_sem.at[j, c],
+            src_ref=src,
+            dst_ref=out_ref.at[j],
+            send_sem=send_sem.at[j, k],
+            recv_sem=recv_sem.at[j],
             device_id=(*kid, q),
             device_id_type=MESH_ID,
         )
 
-    for c in range(WIDE_CHUNKS):
-        for j, (active, is_root, parent, kids) in enumerate(trees):
-            @pl.when(jnp.logical_and(active, jnp.logical_not(is_root)))
-            def _():
-                copy(out_ref.at[j], j, c, 0, (y, x, h)).wait_recv()
+    for j, (active, is_root, parent, kids, depth) in enumerate(trees):
+        root_here = jnp.logical_and(active, is_root)
+
+        for k, (cond, kid) in enumerate(kids):
+            @pl.when(jnp.logical_and(root_here, cond))
+            def _():
+                copy(src_ref, j, k, kid).start()
+
+        @pl.when(root_here)
+        def _():
+            out_ref[j] = src_ref[...]
+
+    for level in range(1, MAX_DEPTH):
+        for j, (active, is_root, parent, kids, depth) in enumerate(trees):
+            here = jnp.logical_and(active, depth == level)
+
+            @pl.when(here)
+            def _():
+                copy(out_ref.at[j], j, 0, (y, x, h)).wait_recv()
 
             for k, (cond, kid) in enumerate(kids):
-                go = jnp.logical_and(active, cond)
-
-                @pl.when(jnp.logical_and(go, is_root))
+                @pl.when(jnp.logical_and(here, cond))
                 def _():
-                    copy(src_ref, j, c, k, kid).start()
-
-                @pl.when(jnp.logical_and(go, jnp.logical_not(is_root)))
-                def _():
-                    copy(out_ref.at[j], j, c, k, kid).start()
-
-    for c in range(WIDE_CHUNKS):
-        for j, (active, is_root, parent, kids) in enumerate(trees):
-            for k, (cond, kid) in enumerate(kids):
-                @pl.when(jnp.logical_and(active, cond))
-                def _():
-                    copy(out_ref.at[j], j, c, k, kid).wait_send()
+                    copy(out_ref.at[j], j, k, kid).start()
+
+    for j, (active, is_root, parent, kids, depth) in enumerate(trees):
+        for k, (cond, kid) in enumerate(kids):
+            @pl.when(jnp.logical_and(active, cond))
+            def _():
+                copy(out_ref.at[j], j, k, kid).wait_send()
 
 
 def wide_bcast(block):
@@ -220,8 +222,8 @@
         in_specs=[pl.BlockSpec(memory_space=pltpu.VMEM)],
         out_specs=pl.BlockSpec(memory_space=pltpu.VMEM),
         scratch_shapes=[
-            pltpu.SemaphoreType.DMA((N_BLOCKS, WIDE_CHUNKS, N_SLOTS)),
-            pltpu.SemaphoreType.DMA((N_BLOCKS, WIDE_CHUNKS)),
+            pltpu.SemaphoreType.DMA((N_BLOCKS, N_SLOTS)),
+            pltpu.SemaphoreType.DMA((N_BLOCKS,)),
         ],
         compiler_params=pltpu.CompilerParams(collective_id=1, has_side_effects=True),
     )(block)
@@ -232,6 +234,19 @@
         a, b, (((1,), (1,)), ((), ())),
         precision=HIGHEST_PRECISION, preferred_element_type=jnp.float32,
     )
+
+
+def mm(a, b):
+    return jnp.dot(a, b, precision=HIGHEST_PRECISION, preferred_element_type=jnp.float32)
+
+
+def triangular_inverse(lower):
+    n = lower.shape[0]
+    eye = jnp.eye(n, dtype=lower.dtype)
+    inverse = eye / jnp.diagonal(lower)[:, None]
+    for _ in range(max(1, (n - 1).bit_length())):
+        inverse = 2 * inverse - mm(inverse, mm(lower, inverse))
+    return inverse
 
 
 def shards(front, child_update, child_map):
@@ -286,9 +301,7 @@
 
     symmetric = jnp.tril(diag_block) + jnp.tril(diag_block, -1).T
     factor_diag = jnp.tril(jnp.linalg.cholesky(symmetric))
-    inverse = lax.linalg.triangular_solve(
-        factor_diag, jnp.eye(PW, dtype=jnp.float32), left_side=True, lower=True
-    )
+    inverse = triangular_inverse(factor_diag)
     own_factor = mm_t(panel, inverse)
     diag_rows = lax.dynamic_slice_in_dim(factor_diag, jnp.minimum(wide_index, 3) * BS, BS)
     top = jnp.where(wide_index * BS < PW, diag_rows, own_factor[:BS])

time: 577 us -> 309 us (0.54)
  the two profiles are of different devices: /device:TPU:254 before, /device:TPU:106 now
where the time goes in v2:
time: 309 us; the launch traced here: 303 us
  Pallas kernels  99.9 us (32%)
  other arithmetic  85 us (28%)
  waiting for transfers between devices  48.5 us (16%)
  matrix products  48.2 us (16%)
  local copies, waits for them, and re-layouts  14.9 us (5%)
  between operations  3.28 us (1%)
    another operation x15, other arithmetic, shards(): factor_diag = jnp.tril(jnp.linalg.cholesky(symmetric))  79.7 us
    pallas_call x1, Pallas kernels, wide_bcast(): pl.pallas_call(wide_bcast_kernel, out_shape=jax.ShapeDtypeStruct((N_BLOCK...  78.2 us
    ppermute x1, waiting for transfers between devices, from_partner(): lax.ppermute(value, axis, [(i, i ^ 1 << distance) for i in range(lax.axis...  48.5 us
    dot_general x18, matrix products, mm(): jnp.dot(a, b, precision=HIGHEST_PRECISION, preferred_element_type=jnp.flo...  33.7 us
    pallas_call x1, Pallas kernels, narrow_bcast(): pl.pallas_call(narrow_bcast_kernel, out_shape=jax.ShapeDtypeStruct(panel....  21.8 us
    dot_general x3, matrix products, mm_t(): lax.dot_general(a, b, (((1,), (1,)), ((), ())), precision=HIGHEST_PRECISI...  6.65 us
  transfers between devices with their start and end apart: 1, of which 1 were waited for; matrix products, arithmetic and copies ran while one was open for 1% of the time, Pallas kernels for 0%

profile of v2, /device:TPU:106, one launch (start us, length us, event | category | flops | bytes accessed | tf_op | source)
XLA Modules:
  0.0 302.9 jit_solution(14821771554200354029)
XLA Ops:
  0.9 2.0 broadcast_select_fusion
  4.2 3.0 %collective-permute-start = (f32[4,128,512]{2,1,0:T(8,128)}, f32[4,128,512]{2,1,0:T(8,128)S(1)}, u32[]{:S(2)}, u32[]{:S(2)}) collective-permute-start(f32[4,128,512]{2,1,0:T(8,128)} %get-tuple-element.7), channel_id=1, source_target_pairs={{0,256},{8,264},{16,272},{24,280},{32,288},{40,296},{48,304},{56,3... | collective-permute-start | bytes 3145736 | tf_op jit(solution)/shard_map/ppermute | solution.py:21
  9.2 48.5 %collective-permute-done = f32[4,128,512]{2,1,0:T(8,128)S(1)} collective-permute-done((f32[4,128,512]{2,1,0:T(8,128)}, f32[4,128,512]{2,1,0:T(8,128)S(1)}, u32[]{:S(2)}, u32[]{:S(2)}) %collective-permute-start) | collective-permute-done | bytes 1048608 | tf_op jit(solution)/shard_map/ppermute | solution.py:21
  61.5 21.8 %shard_map.37 = f32[512,512]{1,0:T(8,128)} custom-call(f32[512,512]{1,0:T(8,128)} %add.209.src_ref), custom_call_target="tpu_custom_call" | custom-call | tf_op jit(solution)/shard_map/pallas_call | solution.py:93
  85.0 78.2 %shard_map.38 = f32[8,128,512]{2,1,0:T(8,128)} custom-call(f32[128,512]{1,0:T(8,128)} %slice.96.src_ref), custom_call_target="tpu_custom_call" | custom-call | tf_op jit(solution)/shard_map/pallas_call | solution.py:219
  169.4 11.7 %cholesky.103 = f32[128,128]{1,0:T(8,128)S(1)} custom-call(f32[128,128]{1,0:T(8,128)S(1)} %cholesky.263), custom_call_target="Cholesky" | custom-call | tf_op jit(solution)/shard_map/jit(cholesky)/cholesky | solution.py:303
  181.3 9.8 %custom-call.27 = f32[1,128,128]{1,2,0:T(8,128)S(1)} custom-call(f32[1,128,128]{2,1,0:T(8,128)S(1)} %get-tuple-element.18), custom_call_target="InvertDiagBlocksLowerTriangular" | custom-call | tf_op jit(solution)/shard_map/jit(cholesky)/cholesky | solution.py:303
  193.6 11.9 %cholesky.215 = f32[128,128]{1,0:T(8,128)S(1)} custom-call(f32[128,128]{1,0:T(8,128)S(1)} %cholesky.267), custom_call_target="Cholesky" | custom-call | tf_op jit(solution)/shard_map/jit(cholesky)/cholesky | solution.py:303
  205.5 9.8 %custom-call.28 = f32[1,128,128]{1,2,0:T(8,128)S(1)} custom-call(f32[1,128,128]{2,1,0:T(8,128)S(1)} %get-tuple-element.15), custom_call_target="InvertDiagBlocksLowerTriangular" | custom-call | tf_op jit(solution)/shard_map/jit(cholesky)/cholesky | solution.py:303
  216.9 11.7 %cholesky.236 = f32[128,128]{1,0:T(8,128)S(1)} custom-call(f32[128,128]{1,0:T(8,128)S(1)} %cholesky.272), custom_call_target="Cholesky" | custom-call | tf_op jit(solution)/shard_map/jit(cholesky)/cholesky | solution.py:303
  228.7 9.8 %custom-call.29 = f32[1,128,128]{1,2,0:T(8,128)S(1)} custom-call(f32[1,128,128]{2,1,0:T(8,128)S(1)} %get-tuple-element.12), custom_call_target="InvertDiagBlocksLowerTriangular" | custom-call | tf_op jit(solution)/shard_map/jit(cholesky)/cholesky | solution.py:303
  239.9 12.1 %cholesky.253 = f32[128,128]{1,0:T(8,128)S(1)} custom-call(f32[128,128]{1,0:T(8,128)S(1)} %convolution_subtract_fusion.12), custom_call_target="Cholesky" | custom-call | tf_op jit(solution)/shard_map/jit(cholesky)/cholesky | solution.py:303
  257.4 4.5 %gather_fusion = f32[512]{0:T(512)S(1)} fusion(f32[512,512]{1,0:T(8,128)S(1)} %select_select_fusion, s32[512]{0:T(512)S(1)} %bitcast.81), kind=kCustom, calls=%fused_computation | custom fusion | bytes 8192 | tf_op jit(solution)/shard_map/jit(diagonal)/cond/branch_0_fun/gather | solution.py:246
  262.0 1.9 fusion.6
  265.7 1.9 fusion.49
  269.4 1.9 fusion.50
  273.1 1.9 fusion.51
  275.0 2.0 convolution_subtract_fusion.6
  277.0 1.9 fusion.52
  280.8 1.9 fusion.53
  286.3 2.1 convolution_subtract_fusion.3
  295.9 1.9 fusion.57
  297.7 1.9 fusion.58
  299.7 2.9 fusion.1
  (62 shorter events, 42.9 us)
Async XLA Ops:
  4.1 3.8 %copy-start.4 = (s32[512]{0:T(512)S(1)}, s32[512]{0:T(512)}, u32[]{:S(2)}) copy-start(s32[512]{0:T(512)} %param.5) | copy-start | bytes 6148
  4.2 53.5 %collective-permute-start = (f32[4,128,512]{2,1,0:T(8,128)}, f32[4,128,512]{2,1,0:T(8,128)S(1)}, u32[]{:S(2)}, u32[]{:S(2)}) collective-permute-start(f32[4,128,512]{2,1,0:T(8,128)} %get-tuple-element.7), channel_id=1, source_target_pairs={{0,256},{8,264},{16,272},{24,280},{32,288},{40,296},{48,304},{56,3... | collective-permute-start | bytes 3145736 | tf_op jit(solution)/shard_map/ppermute | solution.py:21
  58.3 2.0 copy-start.3
  168.4 1.0 copy-start.2
  294.0 1.9 copy-start.1
  297.7 2.0 copy-start
